TPU v7x, 32 devices: a whole 2x2x4 slice. The times are simulated.
32 devices in a mesh: section: 4 (over y, x), student: 2 (over core), dp: 4 (over z).
Axes of the slice: x: 2, y: 2, z: 4, core: 2. Of those that a mesh axis runs over, the one named last changes fastest.
Arguments:
- in_flight: bfloat16 [4, 2, 128, 4096], P('section', 'student'), may hold values from -6 to 6
- segments: int32 [4, 2, 128], P(None, 'student'), may hold values from 0 to 3, never falling along the last dimension, each value on 1 to 64 neighbouring positions
- norm_gain: float32 [4, 4096], P('section'), may hold values from 0.5 to 1.5
- w_qkv: bfloat16 [4, 4096, 3, 1024], P('section', None, None, 'dp')
- w_out: bfloat16 [4, 1024, 4096], P('section', 'dp'), may hold values from -0.1875 to 0.1875
- final_gain: float32 [4096], replicated, may hold values from 0.25 to 1.75
- student_rows: bfloat16 [2, 3, 2, 128, 1024], P('student', None, None, 'dp'), may hold values from -6 to 6
- student_gain: float32 [2, 1024], P('student'), may hold values from 0.5 to 1.5
- w_head: bfloat16 [2, 1024, 4096], P('student', None, 'section'), may hold values from -0.1875 to 0.1875
Outputs:
- advanced: bfloat16 [4, 2, 128, 4096], P('section', 'student', 'dp')
- grad_head: float32 [2, 1024, 4096], P('student', 'dp', 'section')
Inputs may be any that keep to these rules, and one draw needn't show every extreme that they name: `segments`: along a micro-batch's tokens the crop numbers never fall; each of the 4 crops holds 1 to 64 tokens and one holds exactly 64.
All inputs are finite; a program needn't handle non-finite values.
Results may differ from a plain program's by a relative error of at most 0.025.
Values may be sent and summed in bfloat16 or wider, within the bound.
A program may use at most 64 MiB of HBM per device.

v0:
```python
import jax
import jax.numpy as jnp
from jax import lax
from jax.sharding import PartitionSpec as P

HEAD_SIZE = 128
TOK = 128


def shifted(x, axis, by):
    count = lax.axis_size(axis)
    pairs = [(i, i + by) for i in range(count) if 0 <= i + by < count]
    return lax.ppermute(x, axis, pairs)


def broadcast(value, axis, source):
    kept = jnp.where(lax.axis_index(axis) == source, value, 0).astype(value.dtype)
    return lax.psum(kept, axis)


def layer_norm(rows, gain):
    rows = rows.astype(jnp.float32)
    centred = rows - jnp.mean(rows, axis=-1, keepdims=True)
    spread = jnp.mean(centred * centred, axis=-1, keepdims=True)
    return centred * lax.rsqrt(spread + 1e-06) * gain


def attend(state, crops, gain, weights_qkv, weights_out):
    tokens = state.shape[0]
    width = weights_out.shape[0]
    heads = width // HEAD_SIZE
    normed = layer_norm(state, gain).astype(jnp.bfloat16)
    qkv = jnp.dot(normed, weights_qkv, preferred_element_type=jnp.float32).astype(jnp.bfloat16)
    query = qkv[:, :width].reshape(tokens, heads, HEAD_SIZE)
    keys = qkv[:, width : 2 * width].reshape(tokens, heads, HEAD_SIZE)
    values = qkv[:, 2 * width :].reshape(tokens, heads, HEAD_SIZE)
    scores = jnp.einsum(
        "qhd,khd->hqk", query, keys, preferred_element_type=jnp.float32
    ) * HEAD_SIZE ** (-0.5)
    same = crops[:, None] == crops[None, :]
    scores = jnp.where(same[None], scores, -1e30)
    top = jnp.max(scores, axis=-1, keepdims=True)
    expo = jnp.exp(scores - top)
    probs = (expo / jnp.sum(expo, axis=-1, keepdims=True)).astype(jnp.bfloat16)
    mixed = jnp.einsum("hqk,khd->qhd", probs, values, preferred_element_type=jnp.float32).astype(
        jnp.bfloat16
    )
    return jnp.dot(mixed.reshape(tokens, width), weights_out, preferred_element_type=jnp.float32)


def on_device(
    in_flight, segments, norm_gain, w_qkv, w_out, final_gain, student_rows, student_gain, w_head
):
    section = lax.axis_index("section")
    root = lax.axis_size("section") - 1
    share = in_flight.shape[2] // lax.axis_size("dp")
    first_row = lax.axis_index("dp") * share
    ticks = student_rows.shape[1]
    model_width = in_flight.shape[3]
    weights_qkv = w_qkv[0].reshape(model_width, -1)
    weights_out = w_out[0]
    gain = norm_gain[0]
    crop_table = segments[:, 0, :]
    finals = []
    whole = in_flight[0, 0]
    own_rows = lax.dynamic_slice_in_dim(whole, first_row, share, 0)
    for tick in range(ticks):
        if tick > 0:
            whole = lax.all_gather(own_rows, "dp", axis=0, tiled=True)
        crops = lax.dynamic_index_in_dim(crop_table, section - tick, 0, keepdims=False)
        partial_value = attend(whole, crops, gain, weights_qkv, weights_out)
        summed = lax.psum_scatter(
            partial_value.astype(jnp.bfloat16), "dp", scatter_dimension=0, tiled=True
        ).astype(jnp.float32)
        own_rows = (own_rows.astype(jnp.float32) + summed).astype(jnp.bfloat16)
        finals.append(layer_norm(own_rows, final_gain).astype(jnp.bfloat16))
        own_rows = shifted(own_rows, "section", 1)
    advanced = own_rows[None, None]
    finished = jnp.stack(finals)[:, None]
    block = w_head.shape[2]
    block_start = section * block
    columns = lax.all_gather(finished, "student", axis=1, tiled=True)
    spread_rows = broadcast(columns, "section", root)
    targets = lax.dynamic_slice_in_dim(spread_rows, block_start, block, 3)
    student_width = student_rows.shape[4]
    feats = (
        layer_norm(student_rows[0], student_gain[0]).astype(jnp.bfloat16).reshape(-1, student_width)
    )
    pred = jnp.dot(feats, w_head[0], preferred_element_type=jnp.float32)
    err = ((pred - targets.reshape(-1, block).astype(jnp.float32)) * (2.0 / TOK)).astype(
        jnp.bfloat16
    )
    term = lax.dot_general(feats, err, (((0,), (0,)), ((), ())), preferred_element_type=jnp.float32)
    grad = lax.psum_scatter(
        term.astype(jnp.bfloat16), "dp", scatter_dimension=0, tiled=True
    ).astype(jnp.float32)
    return (advanced, grad[None])


def solution(mesh):
    in_specs = (
        P("section", "student", None, None),
        P(None, "student", None),
        P("section", None),
        P("section", None, None, "dp"),
        P("section", "dp", None),
        P(),
        P("student", None, None, "dp", None),
        P("student", None),
        P("student", None, "section"),
    )
    out_specs = (P("section", "student", "dp", None), P("student", "dp", "section"))
    return jax.shard_map(
        on_device, mesh=mesh, in_specs=in_specs, out_specs=out_specs, check_vma=False
    )
```

profile of v0, /device:TPU:0, one launch (start us, length us, event | category | flops | bytes accessed | tf_op | source)
XLA Modules:
  0.0 340.8 jit_solution(15224556704318031938)
XLA Ops:
  8.2 8.9 %copy.23 = bf16[1,4096,3,256]{1,3,2,0:T(8,128)(2,1)} copy(bf16[1,4096,3,256]{3,1,2,0:T(8,128)(2,1)} %param.12) | data formatting | bytes 12582912 | tf_op args[3]
  17.8 5.0 %convolution_convert_fusion.6 = bf16[128,768]{1,0:T(8,128)(2,1)S(1)} fusion(bf16[4096,768]{0,1:T(8,128)(2,1)} %bitcast.129, bf16[1,1,128,4096]{3,2,1,0:T(8,128)(2,1)S(1)} %copy-done.2, f32[4096]{0:T(1024)S(1)} %bitcast.144, f32[128]{0:T(128)S(1)} %add_rsqrt_fusion.6, f32[128]{0:T(128)S(1)} %broadcast_multiply_fusion.6), kind=kOutput, calls=%fused_computation.41 | convolution fusion | flops 808026112 | bytes 7554048 | tf_op jit(solution)/shard_map/dot_general | solution.py:33
  23.4 1.4 convolution_convert_fusion.2
  24.9 30.1 %reduce-scatter.5.cloned.1.call-done = bf16[32,4096]{1,0:T(8,128)(2,1)} async-done(((bf16[128,4096]{1,0:T(8,128)(2,1)}), bf16[32,4096]{1,0:T(8,128)(2,1)}) %reduce-scatter.5.cloned.1.call-update) | async-done | bytes 262160 | tf_op jit(solution)/shard_map/reduce_scatter | solution.py:72
  55.0 1.1 convert_reduce_fusion.5
  56.1 3.4 collective-permute-start
  59.5 5.1 %collective-permute-done = bf16[32,4096]{1,0:T(8,128)(2,1)S(1)} collective-permute-done((bf16[32,4096]{1,0:T(8,128)(2,1)S(1)}, bf16[32,4096]{1,0:T(8,128)(2,1)S(1)}, u32[]{:S(2)}, u32[]{:S(2)}) %collective-permute-start) | collective-permute-done | bytes 262176 | tf_op jit(solution)/shard_map/ppermute | solution.py:13
  65.6 27.8 %all-gather.5.cloned.1.call-done = bf16[128,4096]{1,0:T(8,128)(2,1)} async-done(((bf16[32,4096]{1,0:T(8,128)(2,1)}), bf16[128,4096]{1,0:T(8,128)(2,1)}) %all-gather.5.cloned.1.call-update) | async-done | bytes 1048592 | tf_op jit(solution)/shard_map/all_gather | solution.py:69
  93.4 1.5 convert_reduce_fusion.2
  95.0 1.7 fusion.10
  96.6 5.0 %convolution_convert_fusion.5 = bf16[128,768]{1,0:T(8,128)(2,1)S(1)} fusion(bf16[4096,768]{0,1:T(8,128)(2,1)} %bitcast.130, bf16[128,4096]{1,0:T(8,128)(2,1)S(1)} %copy-done.3, f32[4096]{0:T(1024)S(1)} %bitcast.145, f32[128]{0:T(128)S(1)} %add_rsqrt_fusion.5, f32[128]{0:T(128)S(1)} %broadcast_multiply_fusion.5), kind=kOutput, calls=%fused_computation.40 | convolution fusion | flops 808026112 | bytes 7554048 | tf_op jit(solution)/shard_map/dot_general | solution.py:33
  102.2 1.4 convolution_convert_fusion.1
  103.8 26.8 %reduce-scatter.7.cloned.1.call-done = bf16[32,4096]{1,0:T(8,128)(2,1)} async-done(((bf16[128,4096]{1,0:T(8,128)(2,1)}), bf16[32,4096]{1,0:T(8,128)(2,1)}) %reduce-scatter.7.cloned.1.call-update) | async-done | bytes 262160 | tf_op jit(solution)/shard_map/reduce_scatter | solution.py:72
  130.5 1.1 convert_reduce_fusion.4
  131.7 3.4 collective-permute-start.1
  135.1 5.1 %collective-permute-done.1 = bf16[32,4096]{1,0:T(8,128)(2,1)S(1)} collective-permute-done((bf16[32,4096]{1,0:T(8,128)(2,1)S(1)}, bf16[32,4096]{1,0:T(8,128)(2,1)S(1)}, u32[]{:S(2)}, u32[]{:S(2)}) %collective-permute-start.1) | collective-permute-done | bytes 262176 | tf_op jit(solution)/shard_map/ppermute | solution.py:13
  141.0 27.9 %all-gather.7.cloned.1.call-done = bf16[128,4096]{1,0:T(8,128)(2,1)} async-done(((bf16[32,4096]{1,0:T(8,128)(2,1)}), bf16[128,4096]{1,0:T(8,128)(2,1)}) %all-gather.7.cloned.1.call-update) | async-done | bytes 1048592 | tf_op jit(solution)/shard_map/all_gather | solution.py:69
  168.9 1.5 convert_reduce_fusion.1
  170.5 1.7 fusion.7
  172.1 5.0 %convolution_convert_fusion.4 = bf16[128,768]{1,0:T(8,128)(2,1)S(1)} fusion(bf16[4096,768]{0,1:T(8,128)(2,1)} %bitcast.131, bf16[128,4096]{1,0:T(8,128)(2,1)S(1)} %copy-done.4, f32[128]{0:T(128)S(1)} %add_rsqrt_fusion.4, f32[128]{0:T(128)S(1)} %broadcast_multiply_fusion.4, f32[4096]{0:T(1024)S(1)} %bitcast.146), kind=kOutput, calls=%fused_computation.39 | convolution fusion | flops 808026112 | bytes 7554048 | tf_op jit(solution)/shard_map/dot_general | solution.py:33
  177.7 1.4 convolution_convert_fusion
  179.8 26.2 %reduce-scatter.9.cloned.1.call-done = bf16[32,4096]{1,0:T(8,128)(2,1)} async-done(((bf16[128,4096]{1,0:T(8,128)(2,1)}), bf16[32,4096]{1,0:T(8,128)(2,1)}) %reduce-scatter.9.cloned.1.call-update) | async-done | bytes 262160 | tf_op jit(solution)/shard_map/reduce_scatter | solution.py:72
  206.0 1.1 convert_reduce_fusion.3
  208.8 8.4 %all-gather.9.cloned.1.call-done = bf16[3,64,4096]{2,1,0:T(8,128)(2,1)} async-done(((bf16[3,32,4096]{2,1,0:T(8,128)(2,1)}), bf16[3,64,4096]{2,1,0:T(8,128)(2,1)}) %all-gather.9.cloned.1.call-update) | async-done | bytes 1572880 | tf_op jit(solution)/shard_map/all_gather | solution.py:82
  217.2 1.3 broadcast_select_fusion
  219.7 62.6 %all-reduce.2.cloned.1.call-done = bf16[3,2,32,4096]{3,2,1,0:T(8,128)(2,1)} async-done(((bf16[3,2,32,4096]{3,2,1,0:T(8,128)(2,1)}), bf16[3,2,32,4096]{3,2,1,0:T(8,128)(2,1)}) %all-reduce.2.cloned.1.call-update) | async-done | bytes 1572880 | tf_op jit(solution)/shard_map/psum | solution.py:18
  282.3 1.0 constant_dynamic-slice_fusion
  283.3 4.1 %convolution_convert_fusion.3 = bf16[1024,1024]{1,0:T(8,128)(2,1)} fusion(bf16[192,1024]{1,0:T(8,128)(2,1)S(1)} %fusion.62, bf16[192,1024]{1,0:T(8,128)(2,1)S(1)} %bitcast.133, bf16[1,1024,1024]{2,1,0:T(8,128)(2,1)} %param.17, bf16[192,1024]{1,0:T(8,128)(2,1)S(1)} %bitcast.134), kind=kOutput, calls=%fused_computation.34 | convolution fusion | flops 807141376 | bytes 5373952 | tf_op jit(solution)/shard_map/dot_general | solution.py:93
  287.4 3.4 collective-permute-start.2
  290.8 5.4 %collective-permute-done.2 = bf16[32,4096]{1,0:T(8,128)(2,1)S(1)} collective-permute-done((bf16[32,4096]{1,0:T(8,128)(2,1)S(1)}, bf16[32,4096]{1,0:T(8,128)(2,1)S(1)}, u32[]{:S(2)}, u32[]{:S(2)}) %collective-permute-start.2) | collective-permute-done | bytes 262176 | tf_op jit(solution)/shard_map/ppermute | solution.py:13
  296.1 35.0 %reduce-scatter.11.cloned.1.call-done = bf16[256,1024]{1,0:T(8,128)(2,1)} async-done(((bf16[1024,1024]{1,0:T(8,128)(2,1)}), bf16[256,1024]{1,0:T(8,128)(2,1)}) %reduce-scatter.11.cloned.1.call-update) | async-done | bytes 524304 | tf_op jit(solution)/shard_map/reduce_scatter | solution.py:94
  331.2 2.1 bitcast_convert_fusion
  (86 shorter events, 9.2 us)
Async XLA Ops:
  7.2 16.2 %copy-start = (bf16[1,256,4096]{2,1,0:T(8,128)(2,1)S(1)}, bf16[1,256,4096]{2,1,0:T(8,128)(2,1)}, u32[]{:S(2)}) copy-start(bf16[1,256,4096]{2,1,0:T(8,128)(2,1)} %param.13) | copy-start | bytes 6291460
  7.2 47.8 %reduce-scatter.5.cloned.1.call-start = ((), (), s32[]{:S(2)}) async-start(), calls=%async_computation.4 | async-start | bytes 1310720 | tf_op jit(solution)/shard_map/reduce_scatter | solution.py:72
  8.2 8.9 %copy-start.2 = (bf16[1,1,128,4096]{3,2,1,0:T(8,128)(2,1)S(1)}, bf16[1,1,128,4096]{3,2,1,0:T(8,128)(2,1)}, u32[]{:S(2)}) copy-start(bf16[1,1,128,4096]{3,2,1,0:T(8,128)(2,1)} %param.9) | copy-start | bytes 3145732
  17.1 0.7 copy-start.11
  24.9 68.6 %all-gather.5.cloned.1.call-start = ((), (), s32[]{:S(2)}) async-start(), calls=%async_computation.5 | async-start | bytes 1310720 | tf_op jit(solution)/shard_map/all_gather | solution.py:69
  56.1 8.5 %collective-permute-start = (bf16[32,4096]{1,0:T(8,128)(2,1)S(1)}, bf16[32,4096]{1,0:T(8,128)(2,1)S(1)}, u32[]{:S(2)}, u32[]{:S(2)}) collective-permute-start(bf16[32,4096]{1,0:T(8,128)(2,1)S(1)} %get-tuple-element.3), channel_id=1, source_target_pairs={{0,8},{8,16},{16,24},{1,9},{9,17},{17,25},{2,10},{10,18},{18,26},{... | collective-permute-start | bytes 786440 | tf_op jit(solution)/shard_map/ppermute | solution.py:13
  64.7 0.7 copy-start.7
  65.4 65.1 %reduce-scatter.7.cloned.1.call-start = ((), (), s32[]{:S(2)}) async-start(), calls=%async_computation.6 | async-start | bytes 1310720 | tf_op jit(solution)/shard_map/reduce_scatter | solution.py:72
  93.4 3.2 copy-start.3
  102.2 28.3 %copy-start.8 = (bf16[32,4096]{1,0:T(8,128)(2,1)S(1)}, bf16[32,4096]{1,0:T(8,128)(2,1)}, u32[]{:S(2)}) copy-start(bf16[32,4096]{1,0:T(8,128)(2,1)} %copy-done.7) | copy-start | bytes 786436
  103.7 65.2 %all-gather.7.cloned.1.call-start = ((), (), s32[]{:S(2)}) async-start(), calls=%async_computation.7 | async-start | bytes 1310720 | tf_op jit(solution)/shard_map/all_gather | solution.py:69
  131.7 8.5 %collective-permute-start.1 = (bf16[32,4096]{1,0:T(8,128)(2,1)S(1)}, bf16[32,4096]{1,0:T(8,128)(2,1)S(1)}, u32[]{:S(2)}, u32[]{:S(2)}) collective-permute-start(bf16[32,4096]{1,0:T(8,128)(2,1)S(1)} %get-tuple-element.5), channel_id=1, source_target_pairs={{0,8},{8,16},{16,24},{1,9},{9,17},{17,25},{2,10},{10,18},{18,26},{... | collective-permute-start | bytes 786440 | tf_op jit(solution)/shard_map/ppermute | solution.py:13
  140.2 0.7 copy-start.5
  140.9 65.1 %reduce-scatter.9.cloned.1.call-start = ((), (), s32[]{:S(2)}) async-start(), calls=%async_computation.8 | async-start | bytes 1310720 | tf_op jit(solution)/shard_map/reduce_scatter | solution.py:72
  168.9 3.2 copy-start.4
  177.7 28.3 %copy-start.6 = (bf16[32,4096]{1,0:T(8,128)(2,1)S(1)}, bf16[32,4096]{1,0:T(8,128)(2,1)}, u32[]{:S(2)}) copy-start(bf16[32,4096]{1,0:T(8,128)(2,1)} %copy-done.5) | copy-start | bytes 786436
  179.2 28.3 %copy-start.9 = (f32[4096]{0:T(1024)S(1)}, f32[4096]{0:T(1024)}, u32[]{:S(2)}) copy-start(f32[4096]{0:T(1024)} %param.14) | copy-start | bytes 49156
  179.2 38.0 %all-gather.9.cloned.1.call-start = ((), (), s32[]{:S(2)}) async-start(), calls=%async_computation.11 | async-start | bytes 2359296 | tf_op jit(solution)/shard_map/all_gather | solution.py:82
  208.8 73.5 %all-reduce.2.cloned.1.call-start = ((), (), s32[]{:S(2)}) async-start(), calls=%async_computation.9 | async-start | bytes 3145728 | tf_op jit(solution)/shard_map/psum | solution.py:18
  208.8 9.7 %copy-start.1 = (bf16[1,3,2,32,1024]{4,3,2,1,0:T(8,128)(2,1)S(1)}, bf16[1,3,2,32,1024]{4,3,2,1,0:T(8,128)(2,1)}, u32[]{:S(2)}) copy-start(bf16[1,3,2,32,1024]{4,3,2,1,0:T(8,128)(2,1)} %param.15) | copy-start | bytes 1179652
  208.8 10.3 %copy-start.10 = (f32[1,1024]{1,0:T(1,128)S(1)}, f32[1,1024]{1,0:T(1,128)}, u32[]{:S(2)}) copy-start(f32[1,1024]{1,0:T(1,128)} %param.16) | copy-start | bytes 12292
  218.5 112.7 %reduce-scatter.11.cloned.1.call-start = ((), (), s32[]{:S(2)}) async-start(), calls=%async_computation.10 | async-start | bytes 2621440 | tf_op jit(solution)/shard_map/reduce_scatter | solution.py:94
  287.4 8.8 %collective-permute-start.2 = (bf16[32,4096]{1,0:T(8,128)(2,1)S(1)}, bf16[32,4096]{1,0:T(8,128)(2,1)S(1)}, u32[]{:S(2)}, u32[]{:S(2)}) collective-permute-start(bf16[32,4096]{1,0:T(8,128)(2,1)S(1)} %get-tuple-element.7), channel_id=1, source_target_pairs={{0,8},{8,16},{16,24},{1,9},{9,17},{17,25},{2,10},{10,18},{18,26},{... | collective-permute-start | bytes 786440 | tf_op jit(solution)/shard_map/ppermute | solution.py:13
Sparse Core Ops, SparseCore 0:
  25.0 29.9 reduce-scatter.4
  65.5 27.8 all-gather.4
  103.8 26.6 reduce-scatter.6
  141.1 27.8 all-gather.6
  179.3 26.6 reduce-scatter.8
  208.9 8.2 all-gather.8
  220.3 61.9 all-reduce.1
  287.5 43.6 reduce-scatter.10
where the time goes:
time: 342 us; the launch traced here: 341 us
  waiting for transfers between devices  261 us (76%)
  matrix products  24.5 us (7%)
  other arithmetic  17.2 us (5%)
  between operations  14.5 us (4%)
  local copies, waits for them, and re-layouts  13.5 us (4%)
  starting transfers between devices  10.5 us (3%)
    reduce_scatter x3, waiting for transfers between devices, on_device(): lax.psum_scatter(partial_value.astype(jnp.bfloat16), 'dp', scatter_dimens...  83.1 us
    psum x1, waiting for transfers between devices, broadcast(): return lax.psum(kept, axis)  62.6 us
    all_gather x2, waiting for transfers between devices, on_device(): whole = lax.all_gather(own_rows, 'dp', axis=0, tiled=True)  55.8 us
    reduce_scatter x1, waiting for transfers between devices, on_device(): lax.psum_scatter(term.astype(jnp.bfloat16), 'dp', scatter_dimension=0, ti...  35 us
    ppermute x3, waiting for transfers between devices, shifted(): return lax.ppermute(x, axis, pairs)  15.6 us
    dot_general x3, matrix products, attend(): jnp.dot(normed, weights_qkv, preferred_element_type=jnp.float32)  15.1 us
    unnamed x29, local copies, waits for them, and re-layouts  11.1 us
    ppermute x3, starting transfers between devices, shifted(): return lax.ppermute(x, axis, pairs)  10.2 us
  transfers between devices with their start and end apart: 11, of which 11 were waited for; matrix products, arithmetic and copies ran while one was open for 0% of the time, Pallas kernels for 0%

commit v1 on v0

--- a/solution.py
+++ b/solution.py
@@ -5,6 +5,28 @@
 
 HEAD_SIZE = 128
 TOK = 128
+
+
+def laid_out(pieces, dim):
+    shape = list(pieces.shape[1:])
+    shape[dim] *= pieces.shape[0]
+    return jnp.moveaxis(pieces, 0, dim).reshape(shape)
+
+
+def gather_around(x, axis, dim):
+    peers = lax.axis_size(axis)
+    pairs = [(i, (i + 1) % peers) for i in range(peers)]
+    back = [(b, a) for a, b in pairs]
+    lower, upper = ([], [])
+    for lap in range(peers - 1):
+        if lap % 2 == 0:
+            lower.append(lax.ppermute(lower[-1] if lower else x, axis, pairs))
+        else:
+            upper.append(lax.ppermute(upper[-1] if upper else x, axis, back))
+    tiles = jnp.stack([*lower[::-1], x, *upper])
+    shift = lax.axis_index(axis) - len(lower)
+    tiles = tiles[(jnp.arange(peers) - shift) % peers]
+    return laid_out(tiles, dim)
 
 
 def shifted(x, axis, by):
@@ -66,7 +88,7 @@
     own_rows = lax.dynamic_slice_in_dim(whole, first_row, share, 0)
     for tick in range(ticks):
         if tick > 0:
-            whole = lax.all_gather(own_rows, "dp", axis=0, tiled=True)
+            whole = gather_around(own_rows, "dp", 0)
         crops = lax.dynamic_index_in_dim(crop_table, section - tick, 0, keepdims=False)
         partial_value = attend(whole, crops, gain, weights_qkv, weights_out)
         summed = lax.psum_scatter(

time: 342 us -> 326 us (0.953)
  waiting for transfers between devices: 261 us -> 235 us
  starting transfers between devices: 10.5 us -> 18.8 us
    all_gather x2 -> x0, waiting for transfers between devices: 55.8 us -> none  [on_device(): whole = lax.all_gather(own_rows, 'dp', axis=0, tiled=True)]
    ppermute x0 -> x6, waiting for transfers between devices: none -> 31.5 us  [the longest x4 27.6 us: gather_around(): lower.append(lax.ppermute(lower[-1] if lower else x, axis, pairs))]
    ppermute x0 -> x6, starting transfers between devices: none -> 8.17 us  [the longest x2 7.69 us: gather_around(): upper.append(lax.ppermute(upper[-1] if upper else x, axis, back))]
    gather x0 -> x2, local copies, waits for them, and re-layouts: none -> 3.67 us  [gather_around(): tiles = tiles[(jnp.arange(peers) - shift) % peers]]
  transfers between devices with their start and end apart: 11 -> 15, of which waited for: 11 -> 15; matrix products, arithmetic and copies ran while one was open for 0% -> 1% of each run, Pallas kernels for 0% -> 0%
where the time goes in v1:
time: 326 us; the launch traced here: 325 us
  waiting for transfers between devices  235 us (72%)
  matrix products  24.5 us (8%)
  starting transfers between devices  18.8 us (6%)
  local copies, waits for them, and re-layouts  16.5 us (5%)
  other arithmetic  15.2 us (5%)
  between operations  14.5 us (4%)
    reduce_scatter x3, waiting for transfers between devices, on_device(): lax.psum_scatter(partial_value.astype(jnp.bfloat16), 'dp', scatter_dimens...  82.4 us
    psum x1, waiting for transfers between devices, broadcast(): return lax.psum(kept, axis)  62.4 us
    reduce_scatter x1, waiting for transfers between devices, on_device(): lax.psum_scatter(term.astype(jnp.bfloat16), 'dp', scatter_dimension=0, ti...  35 us
    ppermute x4, waiting for transfers between devices, gather_around(): lower.append(lax.ppermute(lower[-1] if lower else x, axis, pairs))  27.6 us
    ppermute x3, waiting for transfers between devices, shifted(): return lax.ppermute(x, axis, pairs)  15.7 us
    dot_general x3, matrix products, attend(): jnp.dot(normed, weights_qkv, preferred_element_type=jnp.float32)  15 us
    unnamed x29, local copies, waits for them, and re-layouts  10.4 us
    ppermute x3, starting transfers between devices, shifted(): return lax.ppermute(x, axis, pairs)  10.2 us
  transfers between devices with their start and end apart: 15, of which 15 were waited for; matrix products, arithmetic and copies ran while one was open for 1% of the time, Pallas kernels for 0%

profile of v1, /device:TPU:0, one launch (start us, length us, event | category | flops | bytes accessed | tf_op | source)
XLA Modules:
  0.0 324.9 jit_solution(3429477982972746129)
XLA Ops:
  8.2 8.9 %copy.23 = bf16[1,4096,3,256]{1,3,2,0:T(8,128)(2,1)} copy(bf16[1,4096,3,256]{3,1,2,0:T(8,128)(2,1)} %param.12) | data formatting | bytes 12582912 | tf_op args[3]
  17.8 5.0 %convolution_convert_fusion.6 = bf16[128,768]{1,0:T(8,128)(2,1)S(1)} fusion(bf16[4096,768]{0,1:T(8,128)(2,1)} %bitcast.143, bf16[1,1,128,4096]{3,2,1,0:T(8,128)(2,1)S(1)} %copy-done.2, f32[4096]{0:T(1024)S(1)} %bitcast.160, f32[128]{0:T(128)S(1)} %add_rsqrt_fusion.6, f32[128]{0:T(128)S(1)} %broadcast_multiply_fusion.6), kind=kOutput, calls=%fused_computation.43 | convolution fusion | flops 808026112 | bytes 7554048 | tf_op jit(solution)/shard_map/dot_general | solution.py:55
  23.4 1.4 convolution_convert_fusion.2
  24.9 30.1 %reduce-scatter.5.cloned.1.call-done = bf16[32,4096]{1,0:T(8,128)(2,1)} async-done(((bf16[128,4096]{1,0:T(8,128)(2,1)}), bf16[32,4096]{1,0:T(8,128)(2,1)}) %reduce-scatter.5.cloned.1.call-update) | async-done | bytes 262160 | tf_op jit(solution)/shard_map/reduce_scatter | solution.py:94
  56.1 3.4 %collective-permute-start = (bf16[32,4096]{1,0:T(8,128)(2,1)S(1)}, bf16[32,4096]{1,0:T(8,128)(2,1)S(1)}, u32[]{:S(2)}, u32[]{:S(2)}) collective-permute-start(bf16[32,4096]{1,0:T(8,128)(2,1)S(1)} %get-tuple-element.3), channel_id=1, source_target_pairs={{0,8},{8,16},{16,24},{1,9},{9,17},{17,25},{2,10},{10,18},{18,26},{... | collective-permute-start | bytes 786440 | tf_op jit(solution)/shard_map/ppermute | solution.py:35
  59.5 5.1 %collective-permute-done = bf16[32,4096]{1,0:T(8,128)(2,1)S(1)} collective-permute-done((bf16[32,4096]{1,0:T(8,128)(2,1)S(1)}, bf16[32,4096]{1,0:T(8,128)(2,1)S(1)}, u32[]{:S(2)}, u32[]{:S(2)}) %collective-permute-start) | collective-permute-done | bytes 262176 | tf_op jit(solution)/shard_map/ppermute | solution.py:35
  64.7 3.9 %collective-permute-start.3 = (bf16[32,4096]{1,0:T(8,128)(2,1)S(1)}, bf16[32,4096]{1,0:T(8,128)(2,1)S(1)}, u32[]{:S(2)}, u32[]{:S(2)}) collective-permute-start(bf16[32,4096]{1,0:T(8,128)(2,1)S(1)} %collective-permute-done), channel_id=1, source_target_pairs={{1,0},{2,1},{3,2},{0,3},{5,4},{6,5},{7,6},{4,7},{9,8},{10,9},{11,1... | collective-permute-start | bytes 786440 | tf_op jit(solution)/shard_map/ppermute | solution.py:25
  68.6 7.1 %collective-permute-done.1 = bf16[32,4096]{1,0:T(8,128)(2,1)S(1)} collective-permute-done((bf16[32,4096]{1,0:T(8,128)(2,1)S(1)}, bf16[32,4096]{1,0:T(8,128)(2,1)S(1)}, u32[]{:S(2)}, u32[]{:S(2)}) %collective-permute-start.1) | collective-permute-done | bytes 262176 | tf_op jit(solution)/shard_map/ppermute | solution.py:23
  76.0 2.0 collective-permute-done.3
  78.0 6.6 %collective-permute-done.2 = bf16[32,4096]{1,0:T(8,128)(2,1)S(1)} collective-permute-done((bf16[32,4096]{1,0:T(8,128)(2,1)S(1)}, bf16[32,4096]{1,0:T(8,128)(2,1)S(1)}, u32[]{:S(2)}, u32[]{:S(2)}) %collective-permute-start.2) | collective-permute-done | bytes 262176 | tf_op jit(solution)/shard_map/ppermute | solution.py:23
  85.7 1.8 gather_fusion
  88.6 5.0 %convolution_convert_fusion.5 = bf16[128,768]{1,0:T(8,128)(2,1)S(1)} fusion(bf16[128,4096]{1,0:T(8,128)(2,1)S(1)} %bitcast.148, bf16[4096,768]{0,1:T(8,128)(2,1)} %bitcast.144), kind=kOutput, calls=%fused_computation.42 | convolution fusion | flops 805404672 | bytes 7536640 | tf_op jit(solution)/shard_map/dot_general | solution.py:55
  94.2 1.4 convolution_convert_fusion.1
  95.7 26.5 %reduce-scatter.7.cloned.1.call-done = bf16[32,4096]{1,0:T(8,128)(2,1)} async-done(((bf16[128,4096]{1,0:T(8,128)(2,1)}), bf16[32,4096]{1,0:T(8,128)(2,1)}) %reduce-scatter.7.cloned.1.call-update) | async-done | bytes 262160 | tf_op jit(solution)/shard_map/reduce_scatter | solution.py:94
  124.1 3.4 %collective-permute-start.4 = (bf16[32,4096]{1,0:T(8,128)(2,1)S(1)}, bf16[32,4096]{1,0:T(8,128)(2,1)S(1)}, u32[]{:S(2)}, u32[]{:S(2)}) collective-permute-start(bf16[32,4096]{1,0:T(8,128)(2,1)S(1)} %get-tuple-element.5), channel_id=1, source_target_pairs={{0,8},{8,16},{16,24},{1,9},{9,17},{17,25},{2,10},{10,18},{18,26},{... | collective-permute-start | bytes 786440 | tf_op jit(solution)/shard_map/ppermute | solution.py:35
  127.5 5.1 %collective-permute-done.4 = bf16[32,4096]{1,0:T(8,128)(2,1)S(1)} collective-permute-done((bf16[32,4096]{1,0:T(8,128)(2,1)S(1)}, bf16[32,4096]{1,0:T(8,128)(2,1)S(1)}, u32[]{:S(2)}, u32[]{:S(2)}) %collective-permute-start.4) | collective-permute-done | bytes 262176 | tf_op jit(solution)/shard_map/ppermute | solution.py:35
  132.6 3.8 %collective-permute-start.7 = (bf16[32,4096]{1,0:T(8,128)(2,1)S(1)}, bf16[32,4096]{1,0:T(8,128)(2,1)S(1)}, u32[]{:S(2)}, u32[]{:S(2)}) collective-permute-start(bf16[32,4096]{1,0:T(8,128)(2,1)S(1)} %collective-permute-done.4), channel_id=1, source_target_pairs={{1,0},{2,1},{3,2},{0,3},{5,4},{6,5},{7,6},{4,7},{9,8},{10,9},{11,1... | collective-permute-start | bytes 786440 | tf_op jit(solution)/shard_map/ppermute | solution.py:25
  136.5 7.2 %collective-permute-done.5 = bf16[32,4096]{1,0:T(8,128)(2,1)S(1)} collective-permute-done((bf16[32,4096]{1,0:T(8,128)(2,1)S(1)}, bf16[32,4096]{1,0:T(8,128)(2,1)S(1)}, u32[]{:S(2)}, u32[]{:S(2)}) %collective-permute-start.5) | collective-permute-done | bytes 262176 | tf_op jit(solution)/shard_map/ppermute | solution.py:23
  143.8 1.9 collective-permute-done.7
  145.7 6.8 %collective-permute-done.6 = bf16[32,4096]{1,0:T(8,128)(2,1)S(1)} collective-permute-done((bf16[32,4096]{1,0:T(8,128)(2,1)S(1)}, bf16[32,4096]{1,0:T(8,128)(2,1)S(1)}, u32[]{:S(2)}, u32[]{:S(2)}) %collective-permute-start.6) | collective-permute-done | bytes 262176 | tf_op jit(solution)/shard_map/ppermute | solution.py:23
  153.6 1.8 gather_fusion.1
  156.6 5.0 %convolution_convert_fusion.4 = bf16[128,768]{1,0:T(8,128)(2,1)S(1)} fusion(bf16[128,4096]{1,0:T(8,128)(2,1)S(1)} %bitcast.147, bf16[4096,768]{0,1:T(8,128)(2,1)} %bitcast.145), kind=kOutput, calls=%fused_computation.41 | convolution fusion | flops 805404672 | bytes 7536640 | tf_op jit(solution)/shard_map/dot_general | solution.py:55
  162.2 1.4 convolution_convert_fusion
  164.4 25.8 %reduce-scatter.9.cloned.1.call-done = bf16[32,4096]{1,0:T(8,128)(2,1)} async-done(((bf16[128,4096]{1,0:T(8,128)(2,1)}), bf16[32,4096]{1,0:T(8,128)(2,1)}) %reduce-scatter.9.cloned.1.call-update) | async-done | bytes 262160 | tf_op jit(solution)/shard_map/reduce_scatter | solution.py:94
  193.0 8.4 %all-gather.3.cloned.1.call-done = bf16[3,64,4096]{2,1,0:T(8,128)(2,1)} async-done(((bf16[3,32,4096]{2,1,0:T(8,128)(2,1)}), bf16[3,64,4096]{2,1,0:T(8,128)(2,1)}) %all-gather.3.cloned.1.call-update) | async-done | bytes 1572880 | tf_op jit(solution)/shard_map/all_gather | solution.py:104
  201.4 1.3 broadcast_select_fusion
  203.8 62.4 %all-reduce.2.cloned.1.call-done = bf16[3,2,32,4096]{3,2,1,0:T(8,128)(2,1)} async-done(((bf16[3,2,32,4096]{3,2,1,0:T(8,128)(2,1)}), bf16[3,2,32,4096]{3,2,1,0:T(8,128)(2,1)}) %all-reduce.2.cloned.1.call-update) | async-done | bytes 1572880 | tf_op jit(solution)/shard_map/psum | solution.py:40
  267.3 4.1 %convolution_convert_fusion.3 = bf16[1024,1024]{1,0:T(8,128)(2,1)} fusion(bf16[192,1024]{1,0:T(8,128)(2,1)S(1)} %fusion.54, bf16[192,1024]{1,0:T(8,128)(2,1)S(1)} %bitcast.149, bf16[1,1024,1024]{2,1,0:T(8,128)(2,1)} %param.17, bf16[192,1024]{1,0:T(8,128)(2,1)S(1)} %bitcast.150), kind=kOutput, calls=%fused_computation.36 | convolution fusion | flops 807141376 | bytes 5373952 | tf_op jit(solution)/shard_map/dot_general | solution.py:115
  271.4 3.4 %collective-permute-start.8 = (bf16[32,4096]{1,0:T(8,128)(2,1)S(1)}, bf16[32,4096]{1,0:T(8,128)(2,1)S(1)}, u32[]{:S(2)}, u32[]{:S(2)}) collective-permute-start(bf16[32,4096]{1,0:T(8,128)(2,1)S(1)} %get-tuple-element.7), channel_id=1, source_target_pairs={{0,8},{8,16},{16,24},{1,9},{9,17},{17,25},{2,10},{10,18},{18,26},{... | collective-permute-start | bytes 786440 | tf_op jit(solution)/shard_map/ppermute | solution.py:35
  274.8 5.4 %collective-permute-done.8 = bf16[32,4096]{1,0:T(8,128)(2,1)S(1)} collective-permute-done((bf16[32,4096]{1,0:T(8,128)(2,1)S(1)}, bf16[32,4096]{1,0:T(8,128)(2,1)S(1)}, u32[]{:S(2)}, u32[]{:S(2)}) %collective-permute-start.8) | collective-permute-done | bytes 262176 | tf_op jit(solution)/shard_map/ppermute | solution.py:35
  280.2 35.0 %reduce-scatter.11.cloned.1.call-done = bf16[256,1024]{1,0:T(8,128)(2,1)} async-done(((bf16[1024,1024]{1,0:T(8,128)(2,1)}), bf16[256,1024]{1,0:T(8,128)(2,1)}) %reduce-scatter.11.cloned.1.call-update) | async-done | bytes 524304 | tf_op jit(solution)/shard_map/reduce_scatter | solution.py:116
  315.2 2.1 bitcast_convert_fusion
  (100 shorter events, 17.8 us)
Async XLA Ops:
  7.2 16.2 %copy-start = (bf16[1,256,4096]{2,1,0:T(8,128)(2,1)S(1)}, bf16[1,256,4096]{2,1,0:T(8,128)(2,1)}, u32[]{:S(2)}) copy-start(bf16[1,256,4096]{2,1,0:T(8,128)(2,1)} %param.13) | copy-start | bytes 6291460
  7.2 47.8 %reduce-scatter.5.cloned.1.call-start = ((), (), s32[]{:S(2)}) async-start(), calls=%async_computation.4 | async-start | bytes 1310720 | tf_op jit(solution)/shard_map/reduce_scatter | solution.py:94
  8.2 8.9 %copy-start.2 = (bf16[1,1,128,4096]{3,2,1,0:T(8,128)(2,1)S(1)}, bf16[1,1,128,4096]{3,2,1,0:T(8,128)(2,1)}, u32[]{:S(2)}) copy-start(bf16[1,1,128,4096]{3,2,1,0:T(8,128)(2,1)} %param.9) | copy-start | bytes 3145732
  17.1 0.7 copy-start.9
  24.8 97.4 %reduce-scatter.7.cloned.1.call-start = ((), (), s32[]{:S(2)}) async-start(), calls=%async_computation.5 | async-start | bytes 1310720 | tf_op jit(solution)/shard_map/reduce_scatter | solution.py:94
  56.1 8.5 %collective-permute-start = (bf16[32,4096]{1,0:T(8,128)(2,1)S(1)}, bf16[32,4096]{1,0:T(8,128)(2,1)S(1)}, u32[]{:S(2)}, u32[]{:S(2)}) collective-permute-start(bf16[32,4096]{1,0:T(8,128)(2,1)S(1)} %get-tuple-element.3), channel_id=1, source_target_pairs={{0,8},{8,16},{16,24},{1,9},{9,17},{17,25},{2,10},{10,18},{18,26},{... | collective-permute-start | bytes 786440 | tf_op jit(solution)/shard_map/ppermute | solution.py:35
  64.7 19.9 %copy-start.7 = (bf16[32,4096]{1,0:T(8,128)(2,1)}, bf16[32,4096]{1,0:T(8,128)(2,1)S(1)}, u32[]{:S(2)}) copy-start(bf16[32,4096]{1,0:T(8,128)(2,1)S(1)} %collective-permute-done) | copy-start | bytes 786436
  64.7 11.0 %collective-permute-start.1 = (bf16[32,4096]{1,0:T(8,128)(2,1)S(1)}, bf16[32,4096]{1,0:T(8,128)(2,1)S(1)}, u32[]{:S(2)}, u32[]{:S(2)}) collective-permute-start(bf16[32,4096]{1,0:T(8,128)(2,1)S(1)} %collective-permute-done), channel_id=1, source_target_pairs={{0,1},{1,2},{2,3},{3,0},{4,5},{5,6},{6,7},{7,4},{8,9},{9,10},{10,1... | collective-permute-start | bytes 786440 | tf_op jit(solution)/shard_map/ppermute | solution.py:23
  64.7 13.3 %collective-permute-start.3 = (bf16[32,4096]{1,0:T(8,128)(2,1)S(1)}, bf16[32,4096]{1,0:T(8,128)(2,1)S(1)}, u32[]{:S(2)}, u32[]{:S(2)}) collective-permute-start(bf16[32,4096]{1,0:T(8,128)(2,1)S(1)} %collective-permute-done), channel_id=1, source_target_pairs={{1,0},{2,1},{3,2},{0,3},{5,4},{6,5},{7,6},{4,7},{9,8},{10,9},{11,1... | collective-permute-start | bytes 786440 | tf_op jit(solution)/shard_map/ppermute | solution.py:25
  75.7 8.9 %collective-permute-start.2 = (bf16[32,4096]{1,0:T(8,128)(2,1)S(1)}, bf16[32,4096]{1,0:T(8,128)(2,1)S(1)}, u32[]{:S(2)}, u32[]{:S(2)}) collective-permute-start(bf16[32,4096]{1,0:T(8,128)(2,1)S(1)} %collective-permute-done.1), channel_id=1, source_target_pairs={{0,1},{1,2},{2,3},{3,0},{4,5},{5,6},{6,7},{7,4},{8,9},{9,10},{10,1... | collective-permute-start | bytes 786440 | tf_op jit(solution)/shard_map/ppermute | solution.py:23
  94.2 28.1 %copy-start.8 = (bf16[32,4096]{1,0:T(8,128)(2,1)S(1)}, bf16[32,4096]{1,0:T(8,128)(2,1)}, u32[]{:S(2)}) copy-start(bf16[32,4096]{1,0:T(8,128)(2,1)} %copy-done.7) | copy-start | bytes 786436
  95.7 94.5 %reduce-scatter.9.cloned.1.call-start = ((), (), s32[]{:S(2)}) async-start(), calls=%async_computation.6 | async-start | bytes 1310720 | tf_op jit(solution)/shard_map/reduce_scatter | solution.py:94
  123.4 0.7 copy-start.3
  124.1 8.5 %collective-permute-start.4 = (bf16[32,4096]{1,0:T(8,128)(2,1)S(1)}, bf16[32,4096]{1,0:T(8,128)(2,1)S(1)}, u32[]{:S(2)}, u32[]{:S(2)}) collective-permute-start(bf16[32,4096]{1,0:T(8,128)(2,1)S(1)} %get-tuple-element.5), channel_id=1, source_target_pairs={{0,8},{8,16},{16,24},{1,9},{9,17},{17,25},{2,10},{10,18},{18,26},{... | collective-permute-start | bytes 786440 | tf_op jit(solution)/shard_map/ppermute | solution.py:35
  132.6 19.9 %copy-start.5 = (bf16[32,4096]{1,0:T(8,128)(2,1)}, bf16[32,4096]{1,0:T(8,128)(2,1)S(1)}, u32[]{:S(2)}) copy-start(bf16[32,4096]{1,0:T(8,128)(2,1)S(1)} %collective-permute-done.4) | copy-start | bytes 786436
  132.6 11.0 %collective-permute-start.5 = (bf16[32,4096]{1,0:T(8,128)(2,1)S(1)}, bf16[32,4096]{1,0:T(8,128)(2,1)S(1)}, u32[]{:S(2)}, u32[]{:S(2)}) collective-permute-start(bf16[32,4096]{1,0:T(8,128)(2,1)S(1)} %collective-permute-done.4), channel_id=1, source_target_pairs={{0,1},{1,2},{2,3},{3,0},{4,5},{5,6},{6,7},{7,4},{8,9},{9,10},{10,1... | collective-permute-start | bytes 786440 | tf_op jit(solution)/shard_map/ppermute | solution.py:23
  132.6 13.1 %collective-permute-start.7 = (bf16[32,4096]{1,0:T(8,128)(2,1)S(1)}, bf16[32,4096]{1,0:T(8,128)(2,1)S(1)}, u32[]{:S(2)}, u32[]{:S(2)}) collective-permute-start(bf16[32,4096]{1,0:T(8,128)(2,1)S(1)} %collective-permute-done.4), channel_id=1, source_target_pairs={{1,0},{2,1},{3,2},{0,3},{5,4},{6,5},{7,6},{4,7},{9,8},{10,9},{11,1... | collective-permute-start | bytes 786440 | tf_op jit(solution)/shard_map/ppermute | solution.py:25
  143.6 8.9 %collective-permute-start.6 = (bf16[32,4096]{1,0:T(8,128)(2,1)S(1)}, bf16[32,4096]{1,0:T(8,128)(2,1)S(1)}, u32[]{:S(2)}, u32[]{:S(2)}) collective-permute-start(bf16[32,4096]{1,0:T(8,128)(2,1)S(1)} %collective-permute-done.5), channel_id=1, source_target_pairs={{0,1},{1,2},{2,3},{3,0},{4,5},{5,6},{6,7},{7,4},{8,9},{9,10},{10,1... | collective-permute-start | bytes 786440 | tf_op jit(solution)/shard_map/ppermute | solution.py:23
  162.1 2.0 copy-start.4
  162.1 28.1 %copy-start.6 = (bf16[32,4096]{1,0:T(8,128)(2,1)S(1)}, bf16[32,4096]{1,0:T(8,128)(2,1)}, u32[]{:S(2)}) copy-start(bf16[32,4096]{1,0:T(8,128)(2,1)} %copy-done.5) | copy-start | bytes 786436
  163.6 28.0 %copy-start.10 = (f32[4096]{0:T(1024)S(1)}, f32[4096]{0:T(1024)}, u32[]{:S(2)}) copy-start(f32[4096]{0:T(1024)} %param.14) | copy-start | bytes 49156
  163.6 37.8 %all-gather.3.cloned.1.call-start = ((), (), s32[]{:S(2)}) async-start(), calls=%async_computation.9 | async-start | bytes 2359296 | tf_op jit(solution)/shard_map/all_gather | solution.py:104
  192.9 73.4 %all-reduce.2.cloned.1.call-start = ((), (), s32[]{:S(2)}) async-start(), calls=%async_computation.7 | async-start | bytes 3145728 | tf_op jit(solution)/shard_map/psum | solution.py:40
  193.0 9.7 %copy-start.1 = (bf16[1,3,2,32,1024]{4,3,2,1,0:T(8,128)(2,1)S(1)}, bf16[1,3,2,32,1024]{4,3,2,1,0:T(8,128)(2,1)}, u32[]{:S(2)}) copy-start(bf16[1,3,2,32,1024]{4,3,2,1,0:T(8,128)(2,1)} %param.15) | copy-start | bytes 1179652
  193.0 10.3 %copy-start.11 = (f32[1,1024]{1,0:T(1,128)S(1)}, f32[1,1024]{1,0:T(1,128)}, u32[]{:S(2)}) copy-start(f32[1,1024]{1,0:T(1,128)} %param.16) | copy-start | bytes 12292
  202.7 112.5 %reduce-scatter.11.cloned.1.call-start = ((), (), s32[]{:S(2)}) async-start(), calls=%async_computation.8 | async-start | bytes 2621440 | tf_op jit(solution)/shard_map/reduce_scatter | solution.py:116
  271.4 8.8 %collective-permute-start.8 = (bf16[32,4096]{1,0:T(8,128)(2,1)S(1)}, bf16[32,4096]{1,0:T(8,128)(2,1)S(1)}, u32[]{:S(2)}, u32[]{:S(2)}) collective-permute-start(bf16[32,4096]{1,0:T(8,128)(2,1)S(1)} %get-tuple-element.7), channel_id=1, source_target_pairs={{0,8},{8,16},{16,24},{1,9},{9,17},{17,25},{2,10},{10,18},{18,26},{... | collective-permute-start | bytes 786440 | tf_op jit(solution)/shard_map/ppermute | solution.py:35
Sparse Core Ops, SparseCore 0:
  25.0 29.9 reduce-scatter.4
  95.8 26.4 reduce-scatter.6
  163.7 26.4 reduce-scatter.8
  193.0 8.2 all-gather.2
  204.3 61.9 all-reduce.1
  271.5 43.6 reduce-scatter.10
